TPU v7x, 32 devices: a whole 2x2x4 slice. The times are simulated.
32 devices in a mesh: grp: 2 (over y), keys: 4 (over x, core), qry: 4 (over z).
Axes of the slice: x: 2, y: 2, z: 4, core: 2. Of those that a mesh axis runs over, the one named last changes fastest.
Arguments:
- queries: bfloat16 [4096, 8, 128], P(('grp', 'keys', 'qry')), parts along dimension 0, may hold values from -40 to 40, as said below
- cache_keys: bfloat16 [4096, 128], P(('grp', 'keys')), parts along dimension 0, may hold values from -128 to 128, as said below
- cache_values: bfloat16 [4096, 128], P(('grp', 'keys')), parts along dimension 0, may hold values from -24 to 24
- entry: int32 [8, 4], P(('grp', 'keys'), 'qry'), parts along dimension 0, may hold values from 0 to 3
- visits: int32 [8, 4], P(('grp', 'keys'), 'qry'), parts along dimension 0, may hold values from 3 to 4
- doc_length: int32 [2], P('grp'), parts along dimension 0, may hold values from 1025 to 2048
- slot_params: float32 [2048, 256], P(('grp', 'keys', 'qry')), parts along dimension 0, may hold values from -128 to 128, as said below
- first_moment: float32 [2048, 256], P(('grp', 'keys', 'qry')), parts along dimension 0, may hold values from -3 to 3
- second_moment: float32 [2048, 256], P(('grp', 'keys', 'qry')), parts along dimension 0, may hold values from 0.05 to 1
Outputs:
- teacher_out: bfloat16 [4096, 8, 128], P(('grp', 'keys', 'qry')), parts along dimension 0
- slot_grad: float32 [2048, 256], P(('grp', 'keys', 'qry')), parts along dimension 0
- new_params: float32 [2048, 256], P(('grp', 'keys', 'qry')), parts along dimension 0
- new_first: float32 [2048, 256], P(('grp', 'keys', 'qry')), parts along dimension 0
- new_second: float32 [2048, 256], P(('grp', 'keys', 'qry')), parts along dimension 0
- loss: float32 [2], P('grp'), parts along dimension 0
There are 2 independent parts, one for each index of `grp`. A program takes and returns all parts, laid end to end along the dimension named above; each array names one. Nothing has to cross between parts.
Inputs may be any that keep to these rules, and one draw needn't show every extreme that they name: `queries`: query entries stay within the stated range. `cache_keys`: cache key entries stay within the stated range. `slot_params`: slot entries stay within the stated range.
All inputs are finite; a program needn't handle non-finite values.
Results may differ from a plain program's by a relative error of at most 0.0045.
Values may be sent and summed in bfloat16 or wider, within the bound.
No kernel may reach another device: no remote copies, remote signals or barrier semaphores. Data moves between devices by JAX's collectives and lax.ppermute only.
A program may use at most 64 MiB of HBM per device.

v0:
```python
import math
import jax
import jax.numpy as jnp
from jax import lax
from jax.sharding import PartitionSpec as P

NEG = -1e30


def shifted(block, axis, distance):
    devices = range(lax.axis_size(axis))
    route = [((i - distance) % len(devices), i) for i in devices]
    return lax.ppermute(block, axis, route)


def row_scores(left, right):
    return lax.dot_general(
        left, right, (((1,), (1,)), ((), ())), preferred_element_type=jnp.float32
    )


def attend(state, query_blocks, keys, values, shard, length, score_scale):
    block_width = keys.shape[0]
    place = shard * block_width + lax.iota(jnp.int32, block_width)
    live = (place < length)[None, :]

    def one(block_entry):
        query_portion, big, total, acc = block_entry
        logit_score = jnp.where(live, row_scores(query_portion, keys) * score_scale, NEG)
        new_big = jnp.maximum(big, jnp.max(logit_score, axis=1))
        weight = jnp.where(live, jnp.exp(logit_score - new_big[:, None]), 0.0)
        fade = jnp.exp(big - new_big)
        total = total * fade + jnp.sum(weight, axis=1)
        acc = acc * fade[:, None] + jnp.dot(
            weight.astype(jnp.bfloat16), values, preferred_element_type=jnp.float32
        )
        return (new_big, total, acc)

    big, total, acc = state
    return lax.map(one, (query_blocks, big, total, acc))


def student_tile(loop_state, block_entry, student_keys, student_values, score_scale):
    key_gradient, squared_terms = loop_state
    query_portion, target = block_entry
    logit_score = row_scores(query_portion, student_keys) * score_scale
    peak = jnp.max(logit_score, axis=1, keepdims=True)
    weight = jnp.exp(logit_score - peak)
    prob = weight / jnp.sum(weight, axis=1, keepdims=True)
    block_prob = prob.astype(jnp.bfloat16)
    student_output = jnp.dot(block_prob, student_values, preferred_element_type=jnp.float32)
    diff = student_output - target.astype(jnp.float32)
    squared_terms = squared_terms + jnp.sum(diff * diff)
    block_difference = diff.astype(jnp.bfloat16)
    prob_gradient = row_scores(block_difference, student_values)
    inner = jnp.sum(prob * prob_gradient, axis=1, keepdims=True)
    dscore = (prob * (prob_gradient - inner) * score_scale).astype(jnp.bfloat16)
    dkeys = lax.dot_general(
        dscore, query_portion, (((0,), (0,)), ((), ())), preferred_element_type=jnp.float32
    )
    dvals = lax.dot_general(
        block_prob, block_difference, (((0,), (0,)), ((), ())), preferred_element_type=jnp.float32
    )
    key_gradient = key_gradient + jnp.concatenate([dkeys, dvals], axis=1)
    return ((key_gradient, squared_terms), None)


def body(
    queries,
    cache_keys,
    cache_values,
    entry,
    visits,
    doc_length,
    slot_params,
    first_moment,
    second_moment,
):
    shards = lax.axis_size("keys")
    me = lax.axis_index("keys")
    tok, heads, block_width = queries.shape
    rows = tok * heads
    block = math.gcd(rows, 512)
    nblocks = rows // block
    score_scale = 1.0 / math.sqrt(block_width)
    length = doc_length[0]
    query_blocks = queries.reshape(nblocks, block, block_width)
    start = entry[0, 0]
    count = visits[0, 0]
    state = (
        jnp.full((nblocks, block), NEG, jnp.float32),
        jnp.zeros((nblocks, block), jnp.float32),
        jnp.zeros((nblocks, block, block_width), jnp.float32),
    )

    def visit(step, keys, values, loop_state):
        held = jnp.remainder(me - step, shards)
        go = jnp.remainder(-step - start, shards) < count
        return lax.cond(
            go,
            lambda column_index: attend(
                column_index, query_blocks, keys, values, held, length, score_scale
            ),
            lambda column_index: column_index,
            loop_state,
        )

    def turn(step, loop_state):
        keys, values, big, total, acc = loop_state
        big, total, acc = visit(step, keys, values, (big, total, acc))
        keys, values = shifted((keys, values), "keys", 1)
        return (keys, values, big, total, acc)

    keys, values, big, total, acc = lax.fori_loop(
        0, shards - 1, turn, (cache_keys, cache_values) + state
    )
    big, total, acc = visit(shards - 1, keys, values, (big, total, acc))
    teacher_block_list = (acc / total[:, :, None]).astype(jnp.bfloat16)
    teacher_out = teacher_block_list.reshape(tok, heads, block_width)
    copies = slot_params.astype(jnp.bfloat16)
    complete_sum = lax.all_gather(copies, ("keys", "qry"), axis=0, tiled=True)
    student_keys = complete_sum[:, :block_width]
    student_values = complete_sum[:, block_width:]
    initial_state = (jnp.zeros(complete_sum.shape, jnp.float32), jnp.zeros((), jnp.float32))
    (grad_terms, squared_terms), ignored_value = lax.scan(
        lambda column_index, loop_index: student_tile(
            column_index, loop_index, student_keys, student_values, score_scale
        ),
        initial_state,
        (query_blocks, teacher_block_list),
    )
    slot_grad = lax.psum_scatter(grad_terms, ("keys", "qry"), scatter_dimension=0, tiled=True)
    squares_all = lax.psum(squared_terms, ("keys", "qry"))
    loss = (squares_all / (rows * shards * lax.axis_size("qry"))).reshape(1)
    new_first = 0.9 * first_moment + 0.1 * slot_grad
    new_second = 0.95 * second_moment + 0.05 * slot_grad * slot_grad
    new_params = slot_params - 0.02 * new_first / (jnp.sqrt(new_second) + 1e-08)
    return (teacher_out, slot_grad, new_params, new_first, new_second, loss)


def solution(mesh):
    return jax.shard_map(
        body,
        mesh=mesh,
        in_specs=(
            P(("grp", "keys", "qry"), None, None),
            P(("grp", "keys"), None),
            P(("grp", "keys"), None),
            P(("grp", "keys"), "qry"),
            P(("grp", "keys"), "qry"),
            P("grp"),
            P(("grp", "keys", "qry"), None),
            P(("grp", "keys", "qry"), None),
            P(("grp", "keys", "qry"), None),
        ),
        out_specs=(
            P(("grp", "keys", "qry"), None, None),
            P(("grp", "keys", "qry"), None),
            P(("grp", "keys", "qry"), None),
            P(("grp", "keys", "qry"), None),
            P(("grp", "keys", "qry"), None),
            P("grp"),
        ),
        check_vma=False,
    )
```

profile of v0, /device:TPU:0, one launch (start us, length us, event | category | flops | bytes accessed | tf_op | source)
XLA Modules:
  0.0 162.5 jit_solution(8857728833277977669)
XLA Ops:
  9.5 38.7 %all_gather.3 = bf16[1024,256]{1,0:T(8,128)(2,1)S(1)} all-gather(bf16[64,256]{1,0:T(8,128)(2,1)S(1)} %convert_element_type.42), channel_id=1, replica_groups=mesh['grp'=2,'keys'=4,'qry'=4] {'keys','qry'}, dimensions={0}, use_global_device_ids=true | all-gather | bytes 557056 | tf_op jit(solution)/shard_map/all_gather | solution.py:121
  48.3 32.7 %while.82 = (s32[]{:T(128)}, bf16[512,128]{1,0:T(8,128)(2,1)S(1)}, bf16[512,128]{1,0:T(8,128)(2,1)S(1)}, f32[2,512]{1,0:T(2,128)S(1)}, f32[2,512]{1,0:T(2,128)S(...) while((s32[]{:T(128)}, bf16[512,128]{1,0:T(8,128)(2,1)S(1)}, ...), condition=%wide.region_7.8_spmd, body=%wide.region_0.7_spmd.sunk | while | flops 136711200 | bytes 6747030 | solution.py:114
  49.6 1.7 %collective-permute-start.1 = (bf16[512,128]{1,0:T(8,128)(2,1)}, bf16[512,128]{1,0:T(8,128)(2,1)S(1)}, u32[]{:S(2)}, u32[]{:S(2)}) collective-permute-start(bf16[512,128]{1,0:T(8,128)(2,1)} %copy.56), channel_id=1, source_target_pairs={{12,0},{0,4},{4,8},{8,12},{13,1},{1,5},{5,9},{9,13},{14,2},{2,6},{... | collective-permute-start | bytes 393224 | tf_op jit(solution)/shard_map/while/body/eval_jaxpr/ppermute | solution.py:13
  52.6 7.5 %conditional.4 = ((f32[2,512]{1,0:T(2,128)S(1)}, f32[2,512]{1,0:T(2,128)S(1)}, f32[2,512,128]{2,1,0:T(8,128)S(1)})) conditional(s32[]{:T(128)} %convert_element_type.75, (f32[2,512]{1,0:T(2,128)S(1)}, f32[2,512]{1,0:T(2,128)S(1)}, f32[2,512,128]{2,1,0:T(8,128)S(1)}) %tuple.135, (s32[]{:T(128)}, s32[]{:T(128)}, s32[]{:T(128)}, f32[2,512]{1,0:T(2,128)S(1)}, ...), branch_computations={%region_1.1_spmd, %region_2.6_spmd} | conditional | flops 136711184 | bytes 5173698 | solution.py:99
  52.7 7.4 %while.80 = (s32[]{:T(128)}, f32[2,512]{1,0:T(2,128)S(1)}, f32[2,512]{1,0:T(2,128)S(1)}, f32[2,512,128]{2,1,0:T(8,128)S(1)}, f32[2,512]{1,0:T(2,128)S(1)}, /*ind...) while((s32[]{:T(128)}, f32[2,512]{1,0:T(2,128)S(1)}, ...), condition=%wide.region_6.5_spmd.clone, body=%wide.region_3.4_spmd.clone.sunk | while | flops 136711168 | bytes 4108453 | solution.py:40
  53.4 1.2 fusion.104
  54.6 1.4 fusion.106
  58.3 1.4 fusion.106
  63.4 7.5 %conditional.4 = ((f32[2,512]{1,0:T(2,128)S(1)}, f32[2,512]{1,0:T(2,128)S(1)}, f32[2,512,128]{2,1,0:T(8,128)S(1)})) conditional(s32[]{:T(128)} %convert_element_type.75, (f32[2,512]{1,0:T(2,128)S(1)}, f32[2,512]{1,0:T(2,128)S(1)}, f32[2,512,128]{2,1,0:T(8,128)S(1)}) %tuple.135, (s32[]{:T(128)}, s32[]{:T(128)}, s32[]{:T(128)}, f32[2,512]{1,0:T(2,128)S(1)}, ...), branch_computations={%region_1.1_spmd, %region_2.6_spmd} | conditional | flops 136711184 | bytes 5173698 | solution.py:99
  63.4 7.4 %while.80 = (s32[]{:T(128)}, f32[2,512]{1,0:T(2,128)S(1)}, f32[2,512]{1,0:T(2,128)S(1)}, f32[2,512,128]{2,1,0:T(8,128)S(1)}, f32[2,512]{1,0:T(2,128)S(1)}, /*ind...) while((s32[]{:T(128)}, f32[2,512]{1,0:T(2,128)S(1)}, ...), condition=%wide.region_6.5_spmd.clone, body=%wide.region_3.4_spmd.clone.sunk | while | flops 136711168 | bytes 4108453 | solution.py:40
  65.4 1.4 fusion.106
  67.8 1.2 fusion.104
  69.0 1.4 fusion.106
  73.5 7.5 %conditional.4 = ((f32[2,512]{1,0:T(2,128)S(1)}, f32[2,512]{1,0:T(2,128)S(1)}, f32[2,512,128]{2,1,0:T(8,128)S(1)})) conditional(s32[]{:T(128)} %convert_element_type.75, (f32[2,512]{1,0:T(2,128)S(1)}, f32[2,512]{1,0:T(2,128)S(1)}, f32[2,512,128]{2,1,0:T(8,128)S(1)}) %tuple.135, (s32[]{:T(128)}, s32[]{:T(128)}, s32[]{:T(128)}, f32[2,512]{1,0:T(2,128)S(1)}, ...), branch_computations={%region_1.1_spmd, %region_2.6_spmd} | conditional | flops 136711184 | bytes 5173698 | solution.py:99
  73.6 7.4 %while.80 = (s32[]{:T(128)}, f32[2,512]{1,0:T(2,128)S(1)}, f32[2,512]{1,0:T(2,128)S(1)}, f32[2,512,128]{2,1,0:T(8,128)S(1)}, f32[2,512]{1,0:T(2,128)S(1)}, /*ind...) while((s32[]{:T(128)}, f32[2,512]{1,0:T(2,128)S(1)}, ...), condition=%wide.region_6.5_spmd.clone, body=%wide.region_3.4_spmd.clone.sunk | while | flops 136711168 | bytes 4108453 | solution.py:40
  75.5 1.4 fusion.106
  79.2 1.4 fusion.106
  81.0 3.8 %conditional.2 = ((f32[2,512]{1,0:T(2,128)S(1)}, f32[2,512,128]{2,1,0:T(8,128)S(1)})) conditional(s32[]{:T(128)} %convert_element_type.40, (f32[2,512]{1,0:T(2,128)S(1)}, f32[2,512,128]{2,1,0:T(8,128)S(1)}) %tuple.70, (s32[]{:T(128)}, s32[]{:T(128)}, f32[2,512]{1,0:T(2,128)S(1)}, f32[2,512]{1,0:T(2,128)S(1)}, bf16[2,512,128]{2,1,0:T(8,128)(2,1)S(1)}, ...), branch_computations={%region_8.9_spmd, %region_9.14_spmd} | conditional | flops 136711184 | bytes 5159334 | solution.py:99
  81.1 3.7 %while.81 = (s32[]{:T(128)}, f32[2,512]{1,0:T(2,128)S(1)}, f32[2,512,128]{2,1,0:T(8,128)S(1)}, f32[2,512]{1,0:T(2,128)S(1)}, f32[2,512]{1,0:T(2,128)S(1)}, /*ind...) while((s32[]{:T(128)}, f32[2,512]{1,0:T(2,128)S(1)}, ...), condition=%wide.region_13.13_spmd.clone, body=%wide.region_10.12_spmd.clone.sunk | while | flops 136711168 | bytes 4102297 | solution.py:40
  85.0 10.0 %while.83 = (s32[]{:T(128)}, f32[1024,256]{0,1:T(8,128)S(1)}, f32[]{:T(128)}, bf16[2,512,128]{2,1,0:T(8,128)(2,1)S(1)}, bf16[1024,128]{1,0:T(8,128)(2,1)S(1)}, /...) while((s32[]{:T(128)}, f32[1024,256]{0,1:T(8,128)S(1)}, ...), condition=%wide.region_19.20_spmd.clone, body=%wide.region_14.19_spmd.clone.sunk | while | flops 680589824 | bytes 26753152 | solution.py:125
  95.1 1.3 copy.15
  96.4 31.9 %psum.7 = f32[]{:T(128)} all-reduce(f32[]{:T(128)} %get-tuple-element.654), channel_id=1, replica_groups=mesh['grp'=2,'keys'=4,'qry'=4] {'keys','qry'}, use_global_device_ids=true, to_apply=%region_21.22 | all-reduce | flops 1 | bytes 8 | tf_op jit(solution)/shard_map/psum | solution.py:133
  129.0 24.0 %reduce-scatter.2.cloned.1.call-done = f32[64,256]{1,0:T(8,128)} async-done(((f32[1024,256]{1,0:T(8,128)}), f32[64,256]{1,0:T(8,128)}) %reduce-scatter.2.cloned.1.call-update) | async-done | bytes 65552 | tf_op jit(solution)/shard_map/reduce_scatter | solution.py:132
  153.0 1.5 divide_subtract_fusion
  (140 shorter events, 29.0 us)
Async XLA Ops:
  7.2 41.1 %copy-start = (bf16[128,8,128]{2,1,0:T(8,128)(2,1)S(1)}, bf16[128,8,128]{2,1,0:T(8,128)(2,1)}, u32[]{:S(2)}) copy-start(bf16[128,8,128]{2,1,0:T(8,128)(2,1)} %param.21) | copy-start | bytes 786436
  7.2 41.1 %copy-start.1 = (bf16[512,128]{1,0:T(8,128)(2,1)S(1)}, bf16[512,128]{1,0:T(8,128)(2,1)}, u32[]{:S(2)}) copy-start(bf16[512,128]{1,0:T(8,128)(2,1)} %param.22) | copy-start | bytes 393220
  7.2 41.1 %copy-start.2 = (bf16[512,128]{1,0:T(8,128)(2,1)S(1)}, bf16[512,128]{1,0:T(8,128)(2,1)}, u32[]{:S(2)}) copy-start(bf16[512,128]{1,0:T(8,128)(2,1)} %param.23) | copy-start | bytes 393220
  7.2 145.8 %reduce-scatter.2.cloned.1.call-start = ((), (), s32[]{:S(2)}) async-start(), calls=%async_computation.1 | async-start | bytes 1114112 | tf_op jit(solution)/shard_map/reduce_scatter | solution.py:132
  49.0 11.1 %collective-permute-start = (bf16[512,128]{1,0:T(8,128)(2,1)}, bf16[512,128]{1,0:T(8,128)(2,1)S(1)}, u32[]{:S(2)}, u32[]{:S(2)}) collective-permute-start(bf16[512,128]{1,0:T(8,128)(2,1)} %copy.55), channel_id=1, source_target_pairs={{12,0},{0,4},{4,8},{8,12},{13,1},{1,5},{5,9},{9,13},{14,2},{2,6},{... | collective-permute-start | bytes 393224 | tf_op jit(solution)/shard_map/while/body/eval_jaxpr/ppermute | solution.py:13
  49.6 10.5 %collective-permute-start.1 = (bf16[512,128]{1,0:T(8,128)(2,1)}, bf16[512,128]{1,0:T(8,128)(2,1)S(1)}, u32[]{:S(2)}, u32[]{:S(2)}) collective-permute-start(bf16[512,128]{1,0:T(8,128)(2,1)} %copy.56), channel_id=1, source_target_pairs={{12,0},{0,4},{4,8},{8,12},{13,1},{1,5},{5,9},{9,13},{14,2},{2,6},{... | collective-permute-start | bytes 393224 | tf_op jit(solution)/shard_map/while/body/eval_jaxpr/ppermute | solution.py:13
  60.8 10.0 %collective-permute-start = (bf16[512,128]{1,0:T(8,128)(2,1)}, bf16[512,128]{1,0:T(8,128)(2,1)S(1)}, u32[]{:S(2)}, u32[]{:S(2)}) collective-permute-start(bf16[512,128]{1,0:T(8,128)(2,1)} %copy.55), channel_id=1, source_target_pairs={{12,0},{0,4},{4,8},{8,12},{13,1},{1,5},{5,9},{9,13},{14,2},{2,6},{... | collective-permute-start | bytes 393224 | tf_op jit(solution)/shard_map/while/body/eval_jaxpr/ppermute | solution.py:13
  61.5 9.4 %collective-permute-start.1 = (bf16[512,128]{1,0:T(8,128)(2,1)}, bf16[512,128]{1,0:T(8,128)(2,1)S(1)}, u32[]{:S(2)}, u32[]{:S(2)}) collective-permute-start(bf16[512,128]{1,0:T(8,128)(2,1)} %copy.56), channel_id=1, source_target_pairs={{12,0},{0,4},{4,8},{8,12},{13,1},{1,5},{5,9},{9,13},{14,2},{2,6},{... | collective-permute-start | bytes 393224 | tf_op jit(solution)/shard_map/while/body/eval_jaxpr/ppermute | solution.py:13
  71.5 9.5 %collective-permute-start = (bf16[512,128]{1,0:T(8,128)(2,1)}, bf16[512,128]{1,0:T(8,128)(2,1)S(1)}, u32[]{:S(2)}, u32[]{:S(2)}) collective-permute-start(bf16[512,128]{1,0:T(8,128)(2,1)} %copy.55), channel_id=1, source_target_pairs={{12,0},{0,4},{4,8},{8,12},{13,1},{1,5},{5,9},{9,13},{14,2},{2,6},{... | collective-permute-start | bytes 393224 | tf_op jit(solution)/shard_map/while/body/eval_jaxpr/ppermute | solution.py:13
  72.2 8.8 %collective-permute-start.1 = (bf16[512,128]{1,0:T(8,128)(2,1)}, bf16[512,128]{1,0:T(8,128)(2,1)S(1)}, u32[]{:S(2)}, u32[]{:S(2)}) collective-permute-start(bf16[512,128]{1,0:T(8,128)(2,1)} %copy.56), channel_id=1, source_target_pairs={{12,0},{0,4},{4,8},{8,12},{13,1},{1,5},{5,9},{9,13},{14,2},{2,6},{... | collective-permute-start | bytes 393224 | tf_op jit(solution)/shard_map/while/body/eval_jaxpr/ppermute | solution.py:13
  95.0 59.5 %copy-start.3 = (bf16[2,512,128]{2,1,0:T(8,128)(2,1)}, bf16[2,512,128]{2,1,0:T(8,128)(2,1)S(1)}, u32[]{:S(2)}) copy-start(bf16[2,512,128]{2,1,0:T(8,128)(2,1)S(1)} %get-tuple-element.1306) | copy-start | bytes 786436
  95.0 58.0 %copy-start.4 = (f32[64,256]{1,0:T(8,128)S(1)}, f32[64,256]{1,0:T(8,128)}, u32[]{:S(2)}) copy-start(f32[64,256]{1,0:T(8,128)} %param.27) | copy-start | bytes 196612
  95.0 57.9 %copy-start.5 = (f32[64,256]{1,0:T(8,128)S(1)}, f32[64,256]{1,0:T(8,128)}, u32[]{:S(2)}) copy-start(f32[64,256]{1,0:T(8,128)} %param.28) | copy-start | bytes 196612
  95.1 57.9 %copy-start.6 = (f32[64,256]{1,0:T(8,128)S(1)}, f32[64,256]{1,0:T(8,128)}, u32[]{:S(2)}) copy-start(f32[64,256]{1,0:T(8,128)} %param.29) | copy-start | bytes 196612
Sparse Core Ops, SparseCore 0:
  96.5 56.4 reduce-scatter.1
where the time goes:
time: 163 us
  blocking collectives  70.6 us (43%)
  waiting for transfers between devices  24.1 us (15%)
  matrix products  23.3 us (14%)
  between operations  17.3 us (11%)
  other arithmetic  12.6 us (8%)
  loops' own time  6.18 us (4%)
  local copies, waits for them, and re-layouts  6.17 us (4%)
  starting transfers between devices  2.3 us (1%)
    all_gather x1, blocking collectives, body(): complete_sum = lax.all_gather(copies, ('keys', 'qry'), axis=0, tiled=True)  38.7 us
    psum x1, blocking collectives, body(): squares_all = lax.psum(squared_terms, ('keys', 'qry'))  31.9 us
    reduce_scatter x1, waiting for transfers between devices, body(): lax.psum_scatter(grad_terms, ('keys', 'qry'), scatter_dimension=0, tiled=...  24 us
    dot_general x12, matrix products, row_scores(): lax.dot_general(left, right, (((1,), (1,)), ((), ())), preferred_element_...  10.1 us
    dot_general x8, matrix products, one(): jnp.dot(weight.astype(jnp.bfloat16), values, preferred_element_type=jnp.f...  9.39 us
    lt x8, other arithmetic, attend(): live = (place < length)[None, :]  5.37 us
    another operation x1, loops' own time, body(): lax.fori_loop(0, shards - 1, turn, (cache_keys, cache_values) + state)  4.07 us
    another operation x8, local copies, waits for them, and re-layouts  3.92 us
  transfers between devices with their start and end apart: 7, of which 1 were waited for; matrix products, arithmetic and copies ran while one was open for 15% of the time, Pallas kernels for 0%

commit v1 on v0

--- a/solution.py
+++ b/solution.py
@@ -118,7 +118,10 @@
     teacher_block_list = (acc / total[:, :, None]).astype(jnp.bfloat16)
     teacher_out = teacher_block_list.reshape(tok, heads, block_width)
     copies = slot_params.astype(jnp.bfloat16)
-    complete_sum = lax.all_gather(copies, ("keys", "qry"), axis=0, tiled=True)
+    devices_2 = lax.axis_size(("keys", "qry"))
+    blocks = jnp.stack([copies for _ in range(devices_2)])
+    blocks = lax.all_to_all(blocks, ("keys", "qry"), split_axis=0, concat_axis=0)
+    complete_sum = jnp.concatenate(blocks, axis=0)
     student_keys = complete_sum[:, :block_width]
     student_values = complete_sum[:, block_width:]
     initial_state = (jnp.zeros(complete_sum.shape, jnp.float32), jnp.zeros((), jnp.float32))

time: 163 us -> 137 us (0.84)
  blocking collectives: 70.6 us -> 35.4 us
  starting transfers between devices: 2.3 us -> 10.1 us
  local copies, waits for them, and re-layouts: 6.17 us -> 8.09 us
    all_gather x1 -> x0, blocking collectives: 38.7 us -> none  [body(): complete_sum = lax.all_gather(copies, ('keys', 'qry'), axis=0, tiled=True)]
    all_to_all x0 -> x1, starting transfers between devices: none -> 7.44 us  [body(): lax.all_to_all(blocks, ('keys', 'qry'), split_axis=0, concat_axis=0)]
    psum x1, blocking collectives: 31.9 us -> 35.4 us  [body(): squares_all = lax.psum(squared_terms, ('keys', 'qry'))]
    another operation x8 -> x9, local copies, waits for them, and re-layouts: 3.92 us -> 4.81 us
  transfers between devices with their start and end apart: 7 -> 8, of which waited for: 1 -> 1; matrix products, arithmetic and copies ran while one was open for 15% -> 22% of each run, Pallas kernels for 0% -> 0%
where the time goes in v1:
time: 137 us; the launch traced here: 136 us
  blocking collectives  35.4 us (26%)
  waiting for transfers between devices  23.4 us (17%)
  matrix products  23.3 us (17%)
  between operations  17.3 us (13%)
  other arithmetic  12.6 us (9%)
  starting transfers between devices  10.1 us (7%)
  local copies, waits for them, and re-layouts  8.09 us (6%)
  loops' own time  6.18 us (5%)
    psum x1, blocking collectives, body(): squares_all = lax.psum(squared_terms, ('keys', 'qry'))  35.4 us
    reduce_scatter x1, waiting for transfers between devices, body(): lax.psum_scatter(grad_terms, ('keys', 'qry'), scatter_dimension=0, tiled=...  23.3 us
    dot_general x12, matrix products, row_scores(): lax.dot_general(left, right, (((1,), (1,)), ((), ())), preferred_element_...  10.1 us
    dot_general x8, matrix products, one(): jnp.dot(weight.astype(jnp.bfloat16), values, preferred_element_type=jnp.f...  9.4 us
    all_to_all x1, starting transfers between devices, body(): lax.all_to_all(blocks, ('keys', 'qry'), split_axis=0, concat_axis=0)  7.44 us
    lt x8, other arithmetic, attend(): live = (place < length)[None, :]  5.37 us
    another operation x1, loops' own time, body(): lax.fori_loop(0, shards - 1, turn, (cache_keys, cache_values) + state)  4.07 us
    another operation x8, local copies, waits for them, and re-layouts  3.95 us
  transfers between devices with their start and end apart: 8, of which 1 were waited for; matrix products, arithmetic and copies ran while one was open for 22% of the time, Pallas kernels for 0%

profile of v1, /device:TPU:0, one launch (start us, length us, event | category | flops | bytes accessed | tf_op | source)
XLA Modules:
  0.0 136.3 jit_solution(1396407432588504097)
XLA Ops:
  9.0 7.4 %all-to-all-start = ((bf16[16,64,256]{2,1,0:T(8,128)(2,1)}), bf16[16,64,256]{2,1,0:T(8,128)(2,1)}, u32[]{:S(2)}, u32[]{:S(2)}) async-start(bf16[16,64,256]{2,1,0:T(8,128)(2,1)} %stack.2), calls=%async_computation | async-start | bytes 1048576 | tf_op jit(solution)/shard_map/all_to_all | solution.py:123
  17.9 33.1 %while.82 = (s32[]{:T(128)}, bf16[512,128]{1,0:T(8,128)(2,1)S(1)}, bf16[512,128]{1,0:T(8,128)(2,1)S(1)}, f32[2,512]{1,0:T(2,128)S(1)}, f32[2,512]{1,0:T(2,128)S(...) while((s32[]{:T(128)}, bf16[512,128]{1,0:T(8,128)(2,1)S(1)}, ...), condition=%wide.region_7.8_spmd, body=%wide.region_0.7_spmd.sunk | while | flops 136711200 | bytes 6747030 | solution.py:114
  19.6 1.6 %collective-permute-start.1 = (bf16[512,128]{1,0:T(8,128)(2,1)}, bf16[512,128]{1,0:T(8,128)(2,1)S(1)}, u32[]{:S(2)}, u32[]{:S(2)}) collective-permute-start(bf16[512,128]{1,0:T(8,128)(2,1)} %copy.56), channel_id=1, source_target_pairs={{12,0},{0,4},{4,8},{8,12},{13,1},{1,5},{5,9},{9,13},{14,2},{2,6},{... | collective-permute-start | bytes 393224 | tf_op jit(solution)/shard_map/while/body/eval_jaxpr/ppermute | solution.py:13
  22.5 7.5 %conditional.4 = ((f32[2,512]{1,0:T(2,128)S(1)}, f32[2,512]{1,0:T(2,128)S(1)}, f32[2,512,128]{2,1,0:T(8,128)S(1)})) conditional(s32[]{:T(128)} %convert_element_type.75, (f32[2,512]{1,0:T(2,128)S(1)}, f32[2,512]{1,0:T(2,128)S(1)}, f32[2,512,128]{2,1,0:T(8,128)S(1)}) %tuple.135, (s32[]{:T(128)}, s32[]{:T(128)}, s32[]{:T(128)}, f32[2,512]{1,0:T(2,128)S(1)}, ...), branch_computations={%region_1.1_spmd, %region_2.6_spmd} | conditional | flops 136711184 | bytes 5173698 | solution.py:99
  22.6 7.4 %while.80 = (s32[]{:T(128)}, f32[2,512]{1,0:T(2,128)S(1)}, f32[2,512]{1,0:T(2,128)S(1)}, f32[2,512,128]{2,1,0:T(8,128)S(1)}, f32[2,512]{1,0:T(2,128)S(1)}, /*ind...) while((s32[]{:T(128)}, f32[2,512]{1,0:T(2,128)S(1)}, ...), condition=%wide.region_6.5_spmd.clone, body=%wide.region_3.4_spmd.clone.sunk | while | flops 136711168 | bytes 4108453 | solution.py:40
  24.5 1.4 %fusion.106 = f32[2,512,128]{2,1,0:T(8,128)S(1)} fusion(f32[2,512,128]{2,1,0:T(8,128)S(1)} %get-tuple-element.1145, s32[]{:T(128)} %get-tuple-element.1142, bf16[512,128]{1,0:T(8,128)(2,1)} %get-tuple-element.1165, f32[512,512]{0,1:T(8,128)S(1)} %get-tuple-element.1107, f32[512]{0:T(512)S(1)} %get-tuple-element.1109, ...), kind=kOutput, calls=%fused_computation.32.clone.1 | convolution fusion | flops 68026368 | bytes 1708548 | tf_op jit(solution)/shard_map/while/body/eval_jaxpr/cond/branch_1_fun/while/body/eval_jaxpr/dot_general | solution.py:34
  26.9 1.2 fusion.104
  28.2 1.4 %fusion.106 = f32[2,512,128]{2,1,0:T(8,128)S(1)} fusion(f32[2,512,128]{2,1,0:T(8,128)S(1)} %get-tuple-element.1145, s32[]{:T(128)} %get-tuple-element.1142, bf16[512,128]{1,0:T(8,128)(2,1)} %get-tuple-element.1165, f32[512,512]{0,1:T(8,128)S(1)} %get-tuple-element.1107, f32[512]{0:T(512)S(1)} %get-tuple-element.1109, ...), kind=kOutput, calls=%fused_computation.32.clone.1 | convolution fusion | flops 68026368 | bytes 1708548 | tf_op jit(solution)/shard_map/while/body/eval_jaxpr/cond/branch_1_fun/while/body/eval_jaxpr/dot_general | solution.py:34
  32.9 7.5 %conditional.4 = ((f32[2,512]{1,0:T(2,128)S(1)}, f32[2,512]{1,0:T(2,128)S(1)}, f32[2,512,128]{2,1,0:T(8,128)S(1)})) conditional(s32[]{:T(128)} %convert_element_type.75, (f32[2,512]{1,0:T(2,128)S(1)}, f32[2,512]{1,0:T(2,128)S(1)}, f32[2,512,128]{2,1,0:T(8,128)S(1)}) %tuple.135, (s32[]{:T(128)}, s32[]{:T(128)}, s32[]{:T(128)}, f32[2,512]{1,0:T(2,128)S(1)}, ...), branch_computations={%region_1.1_spmd, %region_2.6_spmd} | conditional | flops 136711184 | bytes 5173698 | solution.py:99
  33.0 7.4 %while.80 = (s32[]{:T(128)}, f32[2,512]{1,0:T(2,128)S(1)}, f32[2,512]{1,0:T(2,128)S(1)}, f32[2,512,128]{2,1,0:T(8,128)S(1)}, f32[2,512]{1,0:T(2,128)S(1)}, /*ind...) while((s32[]{:T(128)}, f32[2,512]{1,0:T(2,128)S(1)}, ...), condition=%wide.region_6.5_spmd.clone, body=%wide.region_3.4_spmd.clone.sunk | while | flops 136711168 | bytes 4108453 | solution.py:40
  34.9 1.4 %fusion.106 = f32[2,512,128]{2,1,0:T(8,128)S(1)} fusion(f32[2,512,128]{2,1,0:T(8,128)S(1)} %get-tuple-element.1145, s32[]{:T(128)} %get-tuple-element.1142, bf16[512,128]{1,0:T(8,128)(2,1)} %get-tuple-element.1165, f32[512,512]{0,1:T(8,128)S(1)} %get-tuple-element.1107, f32[512]{0:T(512)S(1)} %get-tuple-element.1109, ...), kind=kOutput, calls=%fused_computation.32.clone.1 | convolution fusion | flops 68026368 | bytes 1708548 | tf_op jit(solution)/shard_map/while/body/eval_jaxpr/cond/branch_1_fun/while/body/eval_jaxpr/dot_general | solution.py:34
  37.4 1.2 fusion.104
  38.6 1.4 %fusion.106 = f32[2,512,128]{2,1,0:T(8,128)S(1)} fusion(f32[2,512,128]{2,1,0:T(8,128)S(1)} %get-tuple-element.1145, s32[]{:T(128)} %get-tuple-element.1142, bf16[512,128]{1,0:T(8,128)(2,1)} %get-tuple-element.1165, f32[512,512]{0,1:T(8,128)S(1)} %get-tuple-element.1107, f32[512]{0:T(512)S(1)} %get-tuple-element.1109, ...), kind=kOutput, calls=%fused_computation.32.clone.1 | convolution fusion | flops 68026368 | bytes 1708548 | tf_op jit(solution)/shard_map/while/body/eval_jaxpr/cond/branch_1_fun/while/body/eval_jaxpr/dot_general | solution.py:34
  43.4 7.5 %conditional.4 = ((f32[2,512]{1,0:T(2,128)S(1)}, f32[2,512]{1,0:T(2,128)S(1)}, f32[2,512,128]{2,1,0:T(8,128)S(1)})) conditional(s32[]{:T(128)} %convert_element_type.75, (f32[2,512]{1,0:T(2,128)S(1)}, f32[2,512]{1,0:T(2,128)S(1)}, f32[2,512,128]{2,1,0:T(8,128)S(1)}) %tuple.135, (s32[]{:T(128)}, s32[]{:T(128)}, s32[]{:T(128)}, f32[2,512]{1,0:T(2,128)S(1)}, ...), branch_computations={%region_1.1_spmd, %region_2.6_spmd} | conditional | flops 136711184 | bytes 5173698 | solution.py:99
  43.5 7.4 %while.80 = (s32[]{:T(128)}, f32[2,512]{1,0:T(2,128)S(1)}, f32[2,512]{1,0:T(2,128)S(1)}, f32[2,512,128]{2,1,0:T(8,128)S(1)}, f32[2,512]{1,0:T(2,128)S(1)}, /*ind...) while((s32[]{:T(128)}, f32[2,512]{1,0:T(2,128)S(1)}, ...), condition=%wide.region_6.5_spmd.clone, body=%wide.region_3.4_spmd.clone.sunk | while | flops 136711168 | bytes 4108453 | solution.py:40
  45.5 1.4 %fusion.106 = f32[2,512,128]{2,1,0:T(8,128)S(1)} fusion(f32[2,512,128]{2,1,0:T(8,128)S(1)} %get-tuple-element.1145, s32[]{:T(128)} %get-tuple-element.1142, bf16[512,128]{1,0:T(8,128)(2,1)} %get-tuple-element.1165, f32[512,512]{0,1:T(8,128)S(1)} %get-tuple-element.1107, f32[512]{0:T(512)S(1)} %get-tuple-element.1109, ...), kind=kOutput, calls=%fused_computation.32.clone.1 | convolution fusion | flops 68026368 | bytes 1708548 | tf_op jit(solution)/shard_map/while/body/eval_jaxpr/cond/branch_1_fun/while/body/eval_jaxpr/dot_general | solution.py:34
  49.1 1.4 %fusion.106 = f32[2,512,128]{2,1,0:T(8,128)S(1)} fusion(f32[2,512,128]{2,1,0:T(8,128)S(1)} %get-tuple-element.1145, s32[]{:T(128)} %get-tuple-element.1142, bf16[512,128]{1,0:T(8,128)(2,1)} %get-tuple-element.1165, f32[512,512]{0,1:T(8,128)S(1)} %get-tuple-element.1107, f32[512]{0:T(512)S(1)} %get-tuple-element.1109, ...), kind=kOutput, calls=%fused_computation.32.clone.1 | convolution fusion | flops 68026368 | bytes 1708548 | tf_op jit(solution)/shard_map/while/body/eval_jaxpr/cond/branch_1_fun/while/body/eval_jaxpr/dot_general | solution.py:34
  51.0 3.8 %conditional.2 = ((f32[2,512]{1,0:T(2,128)S(1)}, f32[2,512,128]{2,1,0:T(8,128)S(1)})) conditional(s32[]{:T(128)} %convert_element_type.40, (f32[2,512]{1,0:T(2,128)S(1)}, f32[2,512,128]{2,1,0:T(8,128)S(1)}) %tuple.70, (s32[]{:T(128)}, s32[]{:T(128)}, f32[2,512]{1,0:T(2,128)S(1)}, f32[2,512]{1,0:T(2,128)S(1)}, bf16[2,512,128]{2,1,0:T(8,128)(2,1)S(1)}, ...), branch_computations={%region_8.9_spmd, %region_9.14_spmd} | conditional | flops 136711184 | bytes 5159334 | solution.py:99
  51.0 3.7 %while.81 = (s32[]{:T(128)}, f32[2,512]{1,0:T(2,128)S(1)}, f32[2,512,128]{2,1,0:T(8,128)S(1)}, f32[2,512]{1,0:T(2,128)S(1)}, f32[2,512]{1,0:T(2,128)S(1)}, /*ind...) while((s32[]{:T(128)}, f32[2,512]{1,0:T(2,128)S(1)}, ...), condition=%wide.region_13.13_spmd.clone, body=%wide.region_10.12_spmd.clone.sunk | while | flops 136711168 | bytes 4102297 | solution.py:40
  56.1 10.0 %while.83 = (s32[]{:T(128)}, f32[1024,256]{0,1:T(8,128)S(1)}, f32[]{:T(128)}, bf16[2,512,128]{2,1,0:T(8,128)(2,1)S(1)}, bf16[1024,128]{1,0:T(8,128)(2,1)S(1)}, /...) while((s32[]{:T(128)}, f32[1024,256]{0,1:T(8,128)S(1)}, ...), condition=%wide.region_19.20_spmd.clone, body=%wide.region_14.19_spmd.clone.sunk | while | flops 680589824 | bytes 26753152 | solution.py:128
  66.1 1.3 copy.15
  67.5 35.4 %psum.7 = f32[]{:T(128)} all-reduce(f32[]{:T(128)} %get-tuple-element.654), channel_id=1, replica_groups=mesh['grp'=2,'keys'=4,'qry'=4] {'keys','qry'}, use_global_device_ids=true, to_apply=%region_21.22 | all-reduce | flops 1 | bytes 8 | tf_op jit(solution)/shard_map/psum | solution.py:136
  103.5 23.3 %reduce-scatter.2.cloned.1.call-done = f32[64,256]{1,0:T(8,128)} async-done(((f32[1024,256]{1,0:T(8,128)}), f32[64,256]{1,0:T(8,128)}) %reduce-scatter.2.cloned.1.call-update) | async-done | bytes 65552 | tf_op jit(solution)/shard_map/reduce_scatter | solution.py:135
  126.8 1.5 %divide_subtract_fusion = (f32[64,256]{1,0:T(8,128)}, f32[64,256]{1,0:T(8,128)}, f32[64,256]{1,0:T(8,128)}) fusion(f32[64,256]{1,0:T(8,128)S(1)} %copy-done.4, f32[64,256]{1,0:T(8,128)} %reduce-scatter.2.cloned.1.call-done, f32[64,256]{1,0:T(8,128)S(1)} %copy-done.5, f32[64,256]{1,0:T(8,128)S(1)} %copy-done.6), kind=kLoop, calls=%fused_computation.74 | loop fusion | flops 180224 | bytes 458752 | tf_op jit(solution)/shard_map/sub | solution.py:140
  (142 shorter events, 31.4 us)
Async XLA Ops:
  7.2 10.7 %copy-start = (bf16[128,8,128]{2,1,0:T(8,128)(2,1)S(1)}, bf16[128,8,128]{2,1,0:T(8,128)(2,1)}, u32[]{:S(2)}) copy-start(bf16[128,8,128]{2,1,0:T(8,128)(2,1)} %param.21) | copy-start | bytes 786436
  7.2 10.7 %copy-start.1 = (bf16[512,128]{1,0:T(8,128)(2,1)S(1)}, bf16[512,128]{1,0:T(8,128)(2,1)}, u32[]{:S(2)}) copy-start(bf16[512,128]{1,0:T(8,128)(2,1)} %param.22) | copy-start | bytes 393220
  7.2 10.7 %copy-start.2 = (bf16[512,128]{1,0:T(8,128)(2,1)S(1)}, bf16[512,128]{1,0:T(8,128)(2,1)}, u32[]{:S(2)}) copy-start(bf16[512,128]{1,0:T(8,128)(2,1)} %param.23) | copy-start | bytes 393220
  9.0 46.0 %all-to-all-start = ((bf16[16,64,256]{2,1,0:T(8,128)(2,1)}), bf16[16,64,256]{2,1,0:T(8,128)(2,1)}, u32[]{:S(2)}, u32[]{:S(2)}) async-start(bf16[16,64,256]{2,1,0:T(8,128)(2,1)} %stack.2), calls=%async_computation | async-start | bytes 1048576 | tf_op jit(solution)/shard_map/all_to_all | solution.py:123
  16.4 110.4 %reduce-scatter.2.cloned.1.call-start = ((), (), s32[]{:S(2)}) async-start(), calls=%async_computation.2 | async-start | bytes 1114112 | tf_op jit(solution)/shard_map/reduce_scatter | solution.py:135
  18.6 11.4 %collective-permute-start = (bf16[512,128]{1,0:T(8,128)(2,1)}, bf16[512,128]{1,0:T(8,128)(2,1)S(1)}, u32[]{:S(2)}, u32[]{:S(2)}) collective-permute-start(bf16[512,128]{1,0:T(8,128)(2,1)} %copy.55), channel_id=1, source_target_pairs={{12,0},{0,4},{4,8},{8,12},{13,1},{1,5},{5,9},{9,13},{14,2},{2,6},{... | collective-permute-start | bytes 393224 | tf_op jit(solution)/shard_map/while/body/eval_jaxpr/ppermute | solution.py:13
  19.6 10.5 %collective-permute-start.1 = (bf16[512,128]{1,0:T(8,128)(2,1)}, bf16[512,128]{1,0:T(8,128)(2,1)S(1)}, u32[]{:S(2)}, u32[]{:S(2)}) collective-permute-start(bf16[512,128]{1,0:T(8,128)(2,1)} %copy.56), channel_id=1, source_target_pairs={{12,0},{0,4},{4,8},{8,12},{13,1},{1,5},{5,9},{9,13},{14,2},{2,6},{... | collective-permute-start | bytes 393224 | tf_op jit(solution)/shard_map/while/body/eval_jaxpr/ppermute | solution.py:13
  30.7 9.7 %collective-permute-start = (bf16[512,128]{1,0:T(8,128)(2,1)}, bf16[512,128]{1,0:T(8,128)(2,1)S(1)}, u32[]{:S(2)}, u32[]{:S(2)}) collective-permute-start(bf16[512,128]{1,0:T(8,128)(2,1)} %copy.55), channel_id=1, source_target_pairs={{12,0},{0,4},{4,8},{8,12},{13,1},{1,5},{5,9},{9,13},{14,2},{2,6},{... | collective-permute-start | bytes 393224 | tf_op jit(solution)/shard_map/while/body/eval_jaxpr/ppermute | solution.py:13
  31.5 9.0 %collective-permute-start.1 = (bf16[512,128]{1,0:T(8,128)(2,1)}, bf16[512,128]{1,0:T(8,128)(2,1)S(1)}, u32[]{:S(2)}, u32[]{:S(2)}) collective-permute-start(bf16[512,128]{1,0:T(8,128)(2,1)} %copy.56), channel_id=1, source_target_pairs={{12,0},{0,4},{4,8},{8,12},{13,1},{1,5},{5,9},{9,13},{14,2},{2,6},{... | collective-permute-start | bytes 393224 | tf_op jit(solution)/shard_map/while/body/eval_jaxpr/ppermute | solution.py:13
  41.1 9.8 %collective-permute-start = (bf16[512,128]{1,0:T(8,128)(2,1)}, bf16[512,128]{1,0:T(8,128)(2,1)S(1)}, u32[]{:S(2)}, u32[]{:S(2)}) collective-permute-start(bf16[512,128]{1,0:T(8,128)(2,1)} %copy.55), channel_id=1, source_target_pairs={{12,0},{0,4},{4,8},{8,12},{13,1},{1,5},{5,9},{9,13},{14,2},{2,6},{... | collective-permute-start | bytes 393224 | tf_op jit(solution)/shard_map/while/body/eval_jaxpr/ppermute | solution.py:13
  42.1 8.8 %collective-permute-start.1 = (bf16[512,128]{1,0:T(8,128)(2,1)}, bf16[512,128]{1,0:T(8,128)(2,1)S(1)}, u32[]{:S(2)}, u32[]{:S(2)}) collective-permute-start(bf16[512,128]{1,0:T(8,128)(2,1)} %copy.56), channel_id=1, source_target_pairs={{12,0},{0,4},{4,8},{8,12},{13,1},{1,5},{5,9},{9,13},{14,2},{2,6},{... | collective-permute-start | bytes 393224 | tf_op jit(solution)/shard_map/while/body/eval_jaxpr/ppermute | solution.py:13
  66.1 62.3 %copy-start.3 = (bf16[2,512,128]{2,1,0:T(8,128)(2,1)}, bf16[2,512,128]{2,1,0:T(8,128)(2,1)S(1)}, u32[]{:S(2)}) copy-start(bf16[2,512,128]{2,1,0:T(8,128)(2,1)S(1)} %get-tuple-element.1306) | copy-start | bytes 786436
  66.1 60.8 %copy-start.4 = (f32[64,256]{1,0:T(8,128)S(1)}, f32[64,256]{1,0:T(8,128)}, u32[]{:S(2)}) copy-start(f32[64,256]{1,0:T(8,128)} %param.27) | copy-start | bytes 196612
  66.1 60.8 %copy-start.5 = (f32[64,256]{1,0:T(8,128)S(1)}, f32[64,256]{1,0:T(8,128)}, u32[]{:S(2)}) copy-start(f32[64,256]{1,0:T(8,128)} %param.28) | copy-start | bytes 196612
  66.1 60.7 %copy-start.6 = (f32[64,256]{1,0:T(8,128)S(1)}, f32[64,256]{1,0:T(8,128)}, u32[]{:S(2)}) copy-start(f32[64,256]{1,0:T(8,128)} %param.29) | copy-start | bytes 196612
Sparse Core Ops, SparseCore 0:
  67.6 59.2 reduce-scatter.1
